TPU v7x, 32 devices: a whole 2x2x4 slice. The times are simulated.
32 devices in a mesh: dp: 8 (over z, y), mp: 4 (over x, core).
Axes of the slice: x: 2, y: 2, z: 4, core: 2. Of those that a mesh axis runs over, the one named last changes fastest.
Arguments:
- tokens: bfloat16 [8192, 2048], P('dp'), may hold values from -6 to 6
- out_cot: bfloat16 [8192, 2048], P('dp'), may hold values from -23 to 23
- lengths: int32 [8], P('dp'), may hold values from 1 to 1024, 6144 in all
- seq_family: int32 [8, 1], P('dp'), may hold values from 0 to 3
- family_tokens: int32 [4], replicated, may hold values from 100000 to 3999999
- norm_master: float32 [2048, 6], P('dp'), may hold values from -0.5 to 2.4, as said below
- attn_bias_master: float32 [2, 2048], P(None, 'mp'), may hold values from -2 to 2
- qkv_master: float32 [2048, 3, 2048], P('dp', None, 'mp'), may hold values from -0.125 to 0.125
- proj_master: float32 [2048, 2048], P('dp', 'mp'), may hold values from -1.5 to 1.5
- fc_bias_master: float32 [8192], P('mp'), may hold values from -1.5 to 1.5
- fc_master: float32 [2048, 8192], P('dp', 'mp'), may hold values from -0.125 to 0.125
- down_master: float32 [2048, 8192], P('dp', 'mp'), may hold values from -0.0625 to 0.0625
- norm_moment: float32 [2048, 6], P('dp'), may hold values from -0.0008544922 to 0.0008544922
- attn_bias_moment: float32 [2, 2048], P(None, 'mp'), may hold values from -0.0008544922 to 0.0008544922
- qkv_moment: float32 [2048, 3, 2048], P('dp', None, 'mp'), may hold values from -0.0008544922 to 0.0008544922
- proj_moment: float32 [2048, 2048], P('dp', 'mp'), may hold values from -0.0008544922 to 0.0008544922
- fc_bias_moment: float32 [8192], P('mp'), may hold values from -0.0008544922 to 0.0008544922
- fc_moment: float32 [2048, 8192], P('dp', 'mp'), may hold values from -0.0008544922 to 0.0008544922
- down_moment: float32 [2048, 8192], P('dp', 'mp'), may hold values from -0.0008544922 to 0.0008544922
- norm_average: float32 [2048, 6], P('dp'), may hold values from 0.5 to 1.5
- attn_bias_average: float32 [2, 2048], P(None, 'mp'), may hold values from -2 to 2
- qkv_average: float32 [2048, 3, 2048], P('dp', None, 'mp'), may hold values from -0.125 to 0.125
- proj_average: float32 [2048, 2048], P('dp', 'mp'), may hold values from -1.5 to 1.5
- fc_bias_average: float32 [8192], P('mp'), may hold values from -1.5 to 1.5
- fc_average: float32 [2048, 8192], P('dp', 'mp'), may hold values from -0.125 to 0.125
- down_average: float32 [2048, 8192], P('dp', 'mp'), may hold values from -0.0625 to 0.0625
Outputs:
- block_out: bfloat16 [8192, 2048], P('dp')
- input_grad: float32 [8192, 2048], P('dp')
- norm_grad: float32 [2048, 6], P('dp')
- attn_bias_grad: float32 [2, 2048], P(None, 'mp')
- qkv_grad: float32 [2048, 3, 2048], P('dp', None, 'mp')
- proj_grad: float32 [2048, 2048], P('dp', 'mp')
- fc_bias_grad: float32 [8192], P('mp')
- fc_grad: float32 [2048, 8192], P('dp', 'mp')
- down_grad: float32 [2048, 8192], P('dp', 'mp')
- norm_momentum: float32 [2048, 6], P('dp')
- attn_bias_momentum: float32 [2, 2048], P(None, 'mp')
- qkv_momentum: float32 [2048, 3, 2048], P('dp', None, 'mp')
- proj_momentum: float32 [2048, 2048], P('dp', 'mp')
- fc_bias_momentum: float32 [8192], P('mp')
- fc_momentum: float32 [2048, 8192], P('dp', 'mp')
- down_momentum: float32 [2048, 8192], P('dp', 'mp')
- norm_averaged: float32 [2048, 6], P('dp')
- attn_bias_averaged: float32 [2, 2048], P(None, 'mp')
- qkv_averaged: float32 [2048, 3, 2048], P('dp', None, 'mp')
- proj_averaged: float32 [2048, 2048], P('dp', 'mp')
- fc_bias_averaged: float32 [8192], P('mp')
- fc_averaged: float32 [2048, 8192], P('dp', 'mp')
- down_averaged: float32 [2048, 8192], P('dp', 'mp')
- norm_updated: float32 [2048, 6], P('dp')
- attn_bias_updated: float32 [2, 2048], P(None, 'mp')
- qkv_updated: float32 [2048, 3, 2048], P('dp', None, 'mp')
- proj_updated: float32 [2048, 2048], P('dp', 'mp')
- fc_bias_updated: float32 [8192], P('mp')
- fc_updated: float32 [2048, 8192], P('dp', 'mp')
- down_updated: float32 [2048, 8192], P('dp', 'mp')
- norm_copy: bfloat16 [2048, 6], P('dp')
- attn_bias_copy: bfloat16 [2, 2048], P(None, 'mp')
- qkv_copy: bfloat16 [2048, 3, 2048], P('dp', None, 'mp')
- proj_copy: bfloat16 [2048, 2048], P('dp', 'mp')
- fc_bias_copy: bfloat16 [8192], P('mp')
- fc_copy: bfloat16 [2048, 8192], P('dp', 'mp')
- down_copy: bfloat16 [2048, 8192], P('dp', 'mp')
- grad_norm: float32 [], replicated
Inputs may be any that keep to these rules, and one draw needn't show every extreme that they name: `lengths`: they sum to 6144; the longest is 1024. `seq_family`: every family has a sequence. `norm_master`: gains positive, biases of either sign.
All inputs are finite; a program needn't handle non-finite values. No bound on the sum of `lengths` on one device may be relied on, other than what follows from the above.
Results may differ from a plain program's by a relative error of at most 0.012.
The roundings to bfloat16 on the way count: a program that leaves them out, or rounds other values in their place, can miss the bound.
Values may be sent and summed in bfloat16 or wider, within the bound.
A program may use at most 256 MiB of HBM per device.

v0:
```python
import math
import jax
import jax.numpy as jnp
from jax import lax
from jax.sharding import PartitionSpec as P

HEAD_DIM = 128
LEN = 1024
EPS = 1e-05
MOMENTUM = 0.9
RATE = 192.0
KEEP = 0.9
NEG = -1e30


def layer_norm(value, gain, shift):
    centre = jnp.mean(value, axis=-1, keepdims=True)
    centred = value - centre
    spread = jnp.mean(centred * centred, axis=-1, keepdims=True)
    return centred * lax.rsqrt(spread + EPS) * gain + shift


def gelu_tanh(value):
    return (
        0.5
        * value
        * (1.0 + jnp.tanh(0.7978845608028654 * (value + 0.044715 * value * value * value)))
    )


def local(
    tokens,
    out_cot,
    lengths,
    seq_family,
    family_tokens,
    norm_master,
    attn_bias_master,
    qkv_master,
    proj_master,
    fc_bias_master,
    fc_master,
    down_master,
    norm_moment,
    attn_bias_moment,
    qkv_moment,
    proj_moment,
    fc_bias_moment,
    fc_moment,
    down_moment,
    norm_average,
    attn_bias_average,
    qkv_average,
    proj_average,
    fc_bias_average,
    fc_average,
    down_average,
):
    seq_count = lengths.shape[0]
    row_count = tokens.shape[0]
    seq_len = row_count // seq_count
    family_count = family_tokens.shape[0]
    local_heads = qkv_master.shape[2] // HEAD_DIM
    head_width = qkv_master.shape[2]
    scale = 1.0 / math.sqrt(HEAD_DIM)
    mp_count = lax.axis_size("mp")
    dp_count = lax.axis_size("dp")

    def sum_over_mp(term_fn):
        summed = lax.psum(term_fn(0, row_count), "mp")
        return summed

    family_ids = jnp.arange(family_count, dtype=jnp.int32)
    member = seq_family == family_ids[None, :]
    local_counts = jnp.sum(jnp.where(member, lengths[:, None], 0), axis=0).astype(jnp.float32)
    counts = lax.psum(local_counts, "dp")
    valid_total = jnp.sum(counts)
    share = family_tokens.astype(jnp.float32) / jnp.sum(family_tokens).astype(jnp.float32)
    family_weight = share * valid_total / jnp.maximum(counts, float(LEN // 2))
    seq_weight = jnp.sum(jnp.where(member, family_weight[None, :], 0.0), axis=1)
    places = jnp.arange(seq_len, dtype=jnp.int32)
    token_weight = jnp.where(places[None, :] < lengths[:, None], seq_weight[:, None], 0.0).reshape(
        row_count
    )
    causal = places[:, None] >= places[None, :]
    low_norm = norm_master.astype(jnp.bfloat16)
    low_qkv = qkv_master.astype(jnp.bfloat16)
    low_proj = proj_master.astype(jnp.bfloat16)
    low_fc = fc_master.astype(jnp.bfloat16)
    low_down = down_master.astype(jnp.bfloat16)
    w_qkv, w_proj, w_fc, w_down, w_norm = (
        lax.all_gather(low_qkv, "dp", axis=0, tiled=True),
        lax.all_gather(low_proj, "dp", axis=0, tiled=True),
        lax.all_gather(low_fc, "dp", axis=0, tiled=True),
        lax.all_gather(low_down, "dp", axis=0, tiled=True),
        lax.all_gather(low_norm, "dp", axis=0, tiled=True),
    )
    norm_full = w_norm.astype(jnp.float32)
    bias_rows = jnp.stack(
        [attn_bias_master[0], jnp.zeros_like(attn_bias_master[0]), attn_bias_master[1]], axis=0
    )
    x_in = tokens.astype(jnp.float32)
    ln1_low = layer_norm(x_in, norm_full[:, 0], norm_full[:, 1]).astype(jnp.bfloat16)
    qkv = (
        jnp.einsum("td,dce->tce", ln1_low, w_qkv, preferred_element_type=jnp.float32)
        + bias_rows[None]
    )
    qkv = qkv.astype(jnp.bfloat16)
    heads = qkv.reshape(seq_count, seq_len, 3, local_heads, HEAD_DIM)

    def attend(one_seq):
        query_rows = one_seq[:, 0]
        key_rows = one_seq[:, 1]
        value_rows = one_seq[:, 2]
        scores = (
            jnp.einsum("qhd,khd->hqk", query_rows, key_rows, preferred_element_type=jnp.float32)
            * scale
        )
        scores = jnp.where(causal[None], scores, NEG)
        row_top = jnp.max(scores, axis=-1, keepdims=True)
        log_total = row_top + jnp.log(jnp.sum(jnp.exp(scores - row_top), axis=-1, keepdims=True))
        attn_prob = jnp.exp(scores - log_total).astype(jnp.bfloat16)
        mixed = jnp.einsum(
            "hqk,khd->qhd", attn_prob, value_rows, preferred_element_type=jnp.float32
        )
        return (mixed.astype(jnp.bfloat16), log_total)

    mixed_low, log_kept = lax.map(attend, heads)
    mixed_low = mixed_low.reshape(row_count, head_width)

    def attn_term(start, count):
        return jnp.einsum("te,de->td", mixed_low, w_proj, preferred_element_type=jnp.float32)

    residual_part = x_in + sum_over_mp(attn_term) + norm_full[:, 4]
    ln2_part, ln2_back = jax.vjp(layer_norm, residual_part, norm_full[:, 2], norm_full[:, 3])
    ln2_low = ln2_part.astype(jnp.bfloat16)
    pre_act = (
        jnp.einsum("td,df->tf", ln2_low, w_fc, preferred_element_type=jnp.float32)
        + fc_bias_master[None]
    )
    hidden_act, gelu_back = jax.vjp(gelu_tanh, pre_act)
    hidden_low = hidden_act.astype(jnp.bfloat16)

    def mlp_term(start, count):
        return jnp.einsum("tf,df->td", hidden_low, w_down, preferred_element_type=jnp.float32)

    block_part = (residual_part + sum_over_mp(mlp_term) + norm_full[:, 5]).astype(jnp.bfloat16)
    upstream = token_weight[:, None] * out_cot.astype(jnp.float32)
    upstream_low = upstream.astype(jnp.bfloat16)
    down_sum = jnp.einsum("td,tf->df", upstream_low, hidden_low, preferred_element_type=jnp.float32)
    back_act = jnp.einsum("td,df->tf", upstream_low, w_down, preferred_element_type=jnp.float32)
    back_pre = gelu_back(back_act)[0].astype(jnp.bfloat16)
    fc_bias_sum = jnp.sum(back_pre, axis=0, dtype=jnp.float32)
    fc_sum = jnp.einsum("td,tf->df", ln2_low, back_pre, preferred_element_type=jnp.float32)

    def fc_back_term(start, count):
        return jnp.einsum("tf,df->td", back_pre, w_fc, preferred_element_type=jnp.float32)

    back_ln2 = sum_over_mp(fc_back_term)
    back_resid_part, gain2_sum, shift2_sum = ln2_back(back_ln2)
    back_resid_part = upstream + back_resid_part
    back_attn_low = back_resid_part.astype(jnp.bfloat16)
    proj_sum = jnp.einsum("td,te->de", back_attn_low, mixed_low, preferred_element_type=jnp.float32)
    back_mixed = jnp.einsum(
        "td,de->te", back_attn_low, w_proj, preferred_element_type=jnp.float32
    ).astype(jnp.bfloat16)
    back_mixed = back_mixed.reshape(seq_count, seq_len, local_heads, HEAD_DIM)

    def attend_back(items):
        one_seq, log_total, back_seq = items
        query_rows = one_seq[:, 0]
        key_rows = one_seq[:, 1]
        value_rows = one_seq[:, 2]
        scores = (
            jnp.einsum("qhd,khd->hqk", query_rows, key_rows, preferred_element_type=jnp.float32)
            * scale
        )
        scores = jnp.where(causal[None], scores, NEG)
        attn_prob = jnp.exp(scores - log_total)
        prob_low = attn_prob.astype(jnp.bfloat16)
        back_value = jnp.einsum(
            "hqk,qhd->khd", prob_low, back_seq, preferred_element_type=jnp.float32
        )
        back_prob = jnp.einsum(
            "qhd,khd->hqk", back_seq, value_rows, preferred_element_type=jnp.float32
        )
        back_score = attn_prob * (
            back_prob - jnp.sum(attn_prob * back_prob, axis=-1, keepdims=True)
        )
        back_score = back_score.astype(jnp.bfloat16)
        back_query = (
            jnp.einsum("hqk,khd->qhd", back_score, key_rows, preferred_element_type=jnp.float32)
            * scale
        )
        back_key = (
            jnp.einsum("hqk,qhd->khd", back_score, query_rows, preferred_element_type=jnp.float32)
            * scale
        )
        return jnp.stack([back_query, back_key, back_value], axis=1).astype(jnp.bfloat16)

    back_heads = lax.map(attend_back, (heads, log_kept, back_mixed))
    back_qkv = back_heads.reshape(row_count, 3, head_width)
    attn_bias_sum = jnp.sum(back_qkv[:, 0::2], axis=0, dtype=jnp.float32)
    qkv_sum = jnp.einsum("td,tce->dce", ln1_low, back_qkv, preferred_element_type=jnp.float32)

    def qkv_back_term(start, count):
        return jnp.einsum("tce,dce->td", back_qkv, w_qkv, preferred_element_type=jnp.float32)

    back_ln1 = sum_over_mp(qkv_back_term)
    ln1_again, ln1_back = jax.vjp(layer_norm, x_in, norm_full[:, 0], norm_full[:, 1])
    back_input, gain1_sum, shift1_sum = ln1_back(back_ln1)
    whole = back_resid_part + back_input
    norm_part = jnp.stack(
        [
            gain1_sum,
            shift1_sum,
            gain2_sum,
            shift2_sum,
            jnp.sum(back_resid_part, axis=0),
            jnp.sum(upstream, axis=0),
        ],
        axis=1,
    )
    qkv_reduced, proj_reduced, fc_reduced, down_reduced, norm_reduced = (
        lax.psum_scatter(qkv_sum, "dp", scatter_dimension=0, tiled=True),
        lax.psum_scatter(proj_sum, "dp", scatter_dimension=0, tiled=True),
        lax.psum_scatter(fc_sum, "dp", scatter_dimension=0, tiled=True),
        lax.psum_scatter(down_sum, "dp", scatter_dimension=0, tiled=True),
        lax.psum_scatter(norm_part, "dp", scatter_dimension=0, tiled=True),
    )
    attn_bias_reduced, fc_bias_reduced = lax.psum((attn_bias_sum, fc_bias_sum), "dp")
    raw_grads = [
        reduced / valid_total
        for reduced in (
            norm_reduced,
            attn_bias_reduced,
            qkv_reduced,
            proj_reduced,
            fc_bias_reduced,
            fc_reduced,
            down_reduced,
        )
    ]
    local_squares = jnp.sum(raw_grads[0] * raw_grads[0]) / float(mp_count)
    local_squares = local_squares + jnp.sum(raw_grads[1] * raw_grads[1]) / float(dp_count)
    local_squares = local_squares + jnp.sum(raw_grads[4] * raw_grads[4]) / float(dp_count)
    for grad_raw in (raw_grads[2], raw_grads[3], raw_grads[5], raw_grads[6]):
        local_squares = local_squares + jnp.sum(grad_raw * grad_raw)
    squares = lax.psum(local_squares, ("dp", "mp"))
    grad_norm = jnp.sqrt(squares)
    clip_factor = jnp.minimum(1.0, 1.0 / (grad_norm + 1e-06))
    masters = (
        norm_master,
        attn_bias_master,
        qkv_master,
        proj_master,
        fc_bias_master,
        fc_master,
        down_master,
    )
    moments = (
        norm_moment,
        attn_bias_moment,
        qkv_moment,
        proj_moment,
        fc_bias_moment,
        fc_moment,
        down_moment,
    )
    averages = (
        norm_average,
        attn_bias_average,
        qkv_average,
        proj_average,
        fc_bias_average,
        fc_average,
        down_average,
    )
    grads_out = []
    momenta_out = []
    averaged_out = []
    updated_out = []
    copies_out = []
    for master, moment, average, grad_raw in zip(masters, moments, averages, raw_grads):
        clipped = grad_raw * clip_factor
        momentum = MOMENTUM * moment + clipped
        updated = master - RATE * (clipped + MOMENTUM * momentum)
        averaged = KEEP * average + (1.0 - KEEP) * updated
        grads_out.append(clipped)
        momenta_out.append(momentum)
        averaged_out.append(averaged)
        updated_out.append(updated)
        copies_out.append(updated.astype(jnp.bfloat16))
    return (
        block_part,
        whole,
        grads_out[0],
        grads_out[1],
        grads_out[2],
        grads_out[3],
        grads_out[4],
        grads_out[5],
        grads_out[6],
        momenta_out[0],
        momenta_out[1],
        momenta_out[2],
        momenta_out[3],
        momenta_out[4],
        momenta_out[5],
        momenta_out[6],
        averaged_out[0],
        averaged_out[1],
        averaged_out[2],
        averaged_out[3],
        averaged_out[4],
        averaged_out[5],
        averaged_out[6],
        updated_out[0],
        updated_out[1],
        updated_out[2],
        updated_out[3],
        updated_out[4],
        updated_out[5],
        updated_out[6],
        copies_out[0],
        copies_out[1],
        copies_out[2],
        copies_out[3],
        copies_out[4],
        copies_out[5],
        copies_out[6],
        grad_norm,
    )


def solution(mesh):
    placed = (
        P("dp", None),
        P("dp", None),
        P("dp"),
        P("dp", None),
        P(),
        P("dp", None),
        P(None, "mp"),
        P("dp", None, "mp"),
        P("dp", "mp"),
        P("mp"),
        P("dp", "mp"),
        P("dp", "mp"),
        P("dp", None),
        P(None, "mp"),
        P("dp", None, "mp"),
        P("dp", "mp"),
        P("mp"),
        P("dp", "mp"),
        P("dp", "mp"),
        P("dp", None),
        P(None, "mp"),
        P("dp", None, "mp"),
        P("dp", "mp"),
        P("mp"),
        P("dp", "mp"),
        P("dp", "mp"),
    )
    return jax.shard_map(
        local,
        mesh=mesh,
        in_specs=placed,
        out_specs=(
            P("dp", None),
            P("dp", None),
            P("dp", None),
            P(None, "mp"),
            P("dp", None, "mp"),
            P("dp", "mp"),
            P("mp"),
            P("dp", "mp"),
            P("dp", "mp"),
            P("dp", None),
            P(None, "mp"),
            P("dp", None, "mp"),
            P("dp", "mp"),
            P("mp"),
            P("dp", "mp"),
            P("dp", "mp"),
            P("dp", None),
            P(None, "mp"),
            P("dp", None, "mp"),
            P("dp", "mp"),
            P("mp"),
            P("dp", "mp"),
            P("dp", "mp"),
            P("dp", None),
            P(None, "mp"),
            P("dp", None, "mp"),
            P("dp", "mp"),
            P("mp"),
            P("dp", "mp"),
            P("dp", "mp"),
            P("dp", None),
            P(None, "mp"),
            P("dp", None, "mp"),
            P("dp", "mp"),
            P("mp"),
            P("dp", "mp"),
            P("dp", "mp"),
            P(),
        ),
        check_vma=False,
    )
```

profile of v0, /device:TPU:0, one launch (start us, length us, event | category | flops | bytes accessed | tf_op | source)
XLA Modules:
  0.0 2152.3 jit_solution(12280135592228971859)
XLA Ops:
  19.1 32.9 %all_gather.15 = bf16[2048,6]{0,1:T(8,128)(2,1)S(1)} all-gather(bf16[256,6]{0,1:T(8,128)(2,1)S(1)} %convert_element_type.108), channel_id=1, replica_groups=mesh['dp'=8,'mp'=4] {'dp'}, dimensions={0}, use_global_device_ids=true | all-gather | bytes 27648 | tf_op jit(solution)/shard_map/all_gather | solution.py:96
  52.7 61.0 %all-gather.5.cloned.1.call-done = bf16[2048,3,512]{0,2,1:T(8,128)(2,1)} async-done(((bf16[256,3,512]{0,2,1:T(8,128)(2,1)}), bf16[2048,3,512]{0,2,1:T(8,128)(2,1)}) %all-gather.5.cloned.1.call-update) | async-done | bytes 6291472 | tf_op jit(solution)/shard_map/all_gather | solution.py:92
  113.7 11.1 add_convert_fusion.2
  140.5 23.5 %all-gather.7.cloned.1.call-done = bf16[2048,512]{1,0:T(8,128)(2,1)} async-done(((bf16[256,512]{1,0:T(8,128)(2,1)}), bf16[2048,512]{1,0:T(8,128)(2,1)}) %all-gather.7.cloned.1.call-update) | async-done | bytes 2097168 | tf_op jit(solution)/shard_map/all_gather | solution.py:93
  178.8 18.5 psum.58
  201.1 121.8 %all-reduce.6.cloned.1.call-done = f32[1024,2048]{1,0:T(8,128)} async-done(((f32[1024,2048]{1,0:T(8,128)}), f32[1024,2048]{1,0:T(8,128)}) %all-reduce.6.cloned.1.call-update) | async-done | bytes 8388624 | tf_op jit(solution)/shard_map/psum | solution.py:70
  333.0 117.6 %all-gather.9.cloned.1.call-done = bf16[2048,2048]{1,0:T(8,128)(2,1)} async-done(((bf16[256,2048]{1,0:T(8,128)(2,1)}), bf16[2048,2048]{1,0:T(8,128)(2,1)}) %all-gather.9.cloned.1.call-update) | async-done | bytes 8388624 | tf_op jit(solution)/shard_map/all_gather | solution.py:94
  450.6 15.9 fusion.51
  466.5 109.8 %all-gather.11.cloned.1.call-done = bf16[2048,2048]{1,0:T(8,128)(2,1)} async-done(((bf16[256,2048]{1,0:T(8,128)(2,1)}), bf16[2048,2048]{1,0:T(8,128)(2,1)}) %all-gather.11.cloned.1.call-update) | async-done | bytes 8388624 | tf_op jit(solution)/shard_map/all_gather | solution.py:95
  576.3 21.0 convert_reduce_fusion.1
  610.3 18.3 fusion.49
  628.6 132.9 %all-reduce.8.cloned.1.call-done = f32[1024,2048]{1,0:T(8,128)} async-done(((f32[1024,2048]{1,0:T(8,128)}), f32[1024,2048]{1,0:T(8,128)}) %all-reduce.8.cloned.1.call-update) | async-done | bytes 8388624 | tf_op jit(solution)/shard_map/psum | solution.py:70
  790.7 12.6 multiply_reduce_fusion
  803.3 12.1 multiply_convert_fusion
  844.9 278.3 %all-reduce.10.cloned.1.call-done = (f32[1024,2048]{1,0:T(8,128)}, f32[1024,2048]{1,0:T(8,128)}) async-done(((f32[1024,2048]{1,0:T(8,128)}, f32[1024,2048]{1,0:T(8,128)}), (f32[1024,2048]{1,0:T(8,128)}, f32[1024,2048]{1,0:T(8,128)})) %all-reduce.10.cloned.1.call-update) | async-done | bytes 16777232 | tf_op jit(solution)/shard_map/psum | solution.py:70
  1146.7 13.6 fusion.36
  1161.0 16.4 fusion.50
  1177.7 17.1 fusion.27
  1195.5 37.8 %all-reduce = (f32[2,512]{1,0:T(2,128)S(1)}, f32[2048]{0:T(1024)S(1)}) all-reduce(f32[2,512]{1,0:T(2,128)S(1)} %convert_reduce_fusion.2, f32[2048]{0:T(1024)S(1)} %copy-done.48), channel_id=1, replica_groups=mesh['dp'=8,'mp'=4] {'dp'}, use_global_device_ids=true, to_apply=%region_28.29 | all-reduce | flops 3072 | bytes 24576 | tf_op jit(solution)/shard_map/psum | solution.py:231
  1239.6 41.7 %reduce-scatter.6.cloned.1.call-done = f32[256,6]{0,1:T(8,128)} async-done(((f32[2048,6]{0,1:T(8,128)}), f32[256,6]{0,1:T(8,128)}) %reduce-scatter.6.cloned.1.call-update) | async-done | bytes 6160 | tf_op jit(solution)/shard_map/reduce_scatter | solution.py:229
  1283.9 208.1 %reduce-scatter.8.cloned.1.call-done = f32[256,3,512]{2,0,1:T(8,128)} async-done(((f32[2048,3,512]{2,0,1:T(8,128)}), f32[256,3,512]{2,0,1:T(8,128)}) %reduce-scatter.8.cloned.1.call-update) | async-done | bytes 1572880 | tf_op jit(solution)/shard_map/reduce_scatter | solution.py:225
  1496.3 280.9 %reduce-scatter.12.cloned.1.call-done = f32[256,2048]{1,0:T(8,128)} async-done(((f32[2048,2048]{1,0:T(8,128)}), f32[256,2048]{1,0:T(8,128)}) %reduce-scatter.12.cloned.1.call-update) | async-done | bytes 2097168 | tf_op jit(solution)/shard_map/reduce_scatter | solution.py:227
  1781.3 281.4 %reduce-scatter.14.cloned.1.call-done = f32[256,2048]{1,0:T(8,128)} async-done(((f32[2048,2048]{1,0:T(8,128)}), f32[256,2048]{1,0:T(8,128)}) %reduce-scatter.14.cloned.1.call-update) | async-done | bytes 2097168 | tf_op jit(solution)/shard_map/reduce_scatter | solution.py:228
  2077.0 39.2 %psum.63 = f32[]{:T(128)} all-reduce(f32[]{:T(128)S(6)} %add.249), channel_id=1, replica_groups=mesh['dp'=8,'mp'=4] {'dp','mp'}, use_global_device_ids=true, to_apply=%region_41.42 | all-reduce | flops 1 | bytes 8 | tf_op jit(solution)/shard_map/psum | solution.py:249
  (214 shorter events, 205.2 us)
Async XLA Ops:
  7.2 106.5 %all-gather.5.cloned.1.call-start = ((), (), s32[]{:S(2)}) async-start(), calls=%async_computation.5 | async-start | bytes 7077888 | tf_op jit(solution)/shard_map/all_gather | solution.py:92
  9.9 154.1 %all-gather.7.cloned.1.call-start = ((), (), s32[]{:S(2)}) async-start(), calls=%async_computation.6 | async-start | bytes 2359296 | tf_op jit(solution)/shard_map/all_gather | solution.py:93
  11.7 311.2 %all-reduce.6.cloned.1.call-start = ((), (), s32[]{:S(2)}) async-start(), calls=%async_computation.7 | async-start | bytes 16777216 | tf_op jit(solution)/shard_map/psum | solution.py:70
  15.6 109.2 %copy-start.28 = (f32[1024]{0:T(1024)}, f32[1024]{0:T(1024)S(1)}, u32[]{:S(2)}) copy-start(f32[1024]{0:T(1024)S(1)} %broadcast_multiply_fusion.8) | copy-start | bytes 12292
  19.0 105.8 %copy-start.32 = (f32[1024]{0:T(1024)}, f32[1024]{0:T(1024)S(1)}, u32[]{:S(2)}) copy-start(f32[1024]{0:T(1024)S(1)} %fusion.15) | copy-start | bytes 12292
  19.1 105.8 %copy-start.30 = (f32[1024]{0:T(1024)}, f32[1024]{0:T(1024)S(1)}, u32[]{:S(2)}) copy-start(f32[1024]{0:T(1024)S(1)} %fusion.42) | copy-start | bytes 12292
  52.6 72.3 %copy-start.26 = (f32[2048,1]{0,1:T(1,128)}, f32[2048,1]{0,1:T(1,128)S(1)}, u32[]{:S(2)}) copy-start(f32[2048,1]{0,1:T(1,128)S(1)} %get-tuple-element.123) | copy-start | bytes 24580
  52.6 72.3 %copy-start.46 = (f32[2048,1]{0,1:T(1,128)}, f32[2048,1]{0,1:T(1,128)S(1)}, u32[]{:S(2)}) copy-start(f32[2048,1]{0,1:T(1,128)S(1)} %get-tuple-element.124) | copy-start | bytes 24580
  52.6 398.0 %copy-start.44 = (f32[2048,1]{0,1:T(1,128)}, f32[2048,1]{0,1:T(1,128)S(1)}, u32[]{:S(2)}) copy-start(f32[2048,1]{0,1:T(1,128)S(1)} %get-tuple-element.121) | copy-start | bytes 24580
  171.4 279.2 %all-gather.9.cloned.1.call-start = ((), (), s32[]{:S(2)}) async-start(), calls=%async_computation.8 | async-start | bytes 9437184 | tf_op jit(solution)/shard_map/all_gather | solution.py:94
  174.2 402.1 %all-gather.11.cloned.1.call-start = ((), (), s32[]{:S(2)}) async-start(), calls=%async_computation.9 | async-start | bytes 9437184 | tf_op jit(solution)/shard_map/all_gather | solution.py:95
  177.5 584.0 %all-reduce.8.cloned.1.call-start = ((), (), s32[]{:S(2)}) async-start(), calls=%async_computation.10 | async-start | bytes 16777216 | tf_op jit(solution)/shard_map/psum | solution.py:70
  450.6 125.7 %copy-start.49 = (f32[2048]{0:T(1024)S(1)}, f32[2048]{0:T(1024)}, u32[]{:S(2)}) copy-start(f32[2048]{0:T(1024)} %param.35) | copy-start | bytes 24580
  610.3 513.0 %all-reduce.10.cloned.1.call-start = ((), (), s32[]{:S(2)}) async-start(), calls=%async_computation.16 | async-start | bytes 33554432 | tf_op jit(solution)/shard_map/psum | solution.py:70
  834.1 289.2 %copy-start.27 = (f32[2048,1]{0,1:T(1,128)S(1)}, f32[2048,1]{0,1:T(1,128)}, u32[]{:S(2)}) copy-start(f32[2048,1]{0,1:T(1,128)} %copy-done.26) | copy-start | bytes 24580
  834.1 289.1 %copy-start.29 = (f32[1024]{0:T(1024)S(1)}, f32[1024]{0:T(1024)}, u32[]{:S(2)}) copy-start(f32[1024]{0:T(1024)} %copy-done.28) | copy-start | bytes 12292
  834.1 403.0 %reduce-scatter.10.cloned.1.call-start = ((), (), s32[]{:S(2)}) async-start(), calls=%async_computation.13 | async-start | bytes 4718592 | tf_op jit(solution)/shard_map/reduce_scatter | solution.py:226
  844.8 284.8 %copy-start.33 = (f32[1024]{0:T(1024)S(1)}, f32[1024]{0:T(1024)}, u32[]{:S(2)}) copy-start(f32[1024]{0:T(1024)} %copy-done.32) | copy-start | bytes 12292
  844.8 284.8 %copy-start.31 = (f32[1024]{0:T(1024)S(1)}, f32[1024]{0:T(1024)}, u32[]{:S(2)}) copy-start(f32[1024]{0:T(1024)} %copy-done.30) | copy-start | bytes 12292
  844.9 436.4 %reduce-scatter.6.cloned.1.call-start = ((), (), s32[]{:S(2)}) async-start(), calls=%async_computation.11 | async-start | bytes 73728 | tf_op jit(solution)/shard_map/reduce_scatter | solution.py:229
  1146.5 345.5 %reduce-scatter.8.cloned.1.call-start = ((), (), s32[]{:S(2)}) async-start(), calls=%async_computation.12 | async-start | bytes 14155776 | tf_op jit(solution)/shard_map/reduce_scatter | solution.py:225
  1160.3 616.9 %reduce-scatter.12.cloned.1.call-start = ((), (), s32[]{:S(2)}) async-start(), calls=%async_computation.14 | async-start | bytes 18874368 | tf_op jit(solution)/shard_map/reduce_scatter | solution.py:227
  1177.4 885.3 %reduce-scatter.14.cloned.1.call-start = ((), (), s32[]{:S(2)}) async-start(), calls=%async_computation.15 | async-start | bytes 18874368 | tf_op jit(solution)/shard_map/reduce_scatter | solution.py:228
  1194.8 871.9 %copy-start.34 = (f32[2048,1]{0,1:T(1,128)S(1)}, f32[2048,1]{0,1:T(1,128)}, u32[]{:S(2)}) copy-start(f32[2048,1]{0,1:T(1,128)} %get-tuple-element.119) | copy-start | bytes 24580
  (47 other events, 938.4 us)
Sparse Core Ops, SparseCore 0:
  10.7 102.9 all-gather.4
  116.4 47.5 all-gather.6
  171.5 151.3 all-reduce.5
  325.5 125.0 all-gather.8
  453.1 123.1 all-gather.10
  610.4 151.0 all-reduce.7
  834.2 288.9 all-reduce.9
  1127.5 88.2 reduce-scatter.9
  1220.1 61.1 reduce-scatter.5
  1285.1 206.7 reduce-scatter.7
  1496.2 280.9 reduce-scatter.11
  1780.9 281.7 reduce-scatter.13
where the time goes:
time: 2160 us; the launch traced here: 2150 us
  waiting for transfers between devices  1660 us (77%)
  matrix products  195 us (9%)
  other arithmetic  128 us (6%)
  blocking collectives  128 us (6%)
  between operations  23.6 us (1%)
    psum x3, waiting for transfers between devices, sum_over_mp(): summed = lax.psum(term_fn(0, row_count), 'mp')  533 us
    reduce_scatter x1, waiting for transfers between devices, local(): lax.psum_scatter(down_sum, 'dp', scatter_dimension=0, tiled=True)  281 us
    reduce_scatter x1, waiting for transfers between devices, local(): lax.psum_scatter(fc_sum, 'dp', scatter_dimension=0, tiled=True)  281 us
    reduce_scatter x1, waiting for transfers between devices, local(): lax.psum_scatter(qkv_sum, 'dp', scatter_dimension=0, tiled=True)  208 us
    all_gather x1, waiting for transfers between devices, local(): lax.all_gather(low_fc, 'dp', axis=0, tiled=True)  118 us
    all_gather x1, waiting for transfers between devices, local(): lax.all_gather(low_down, 'dp', axis=0, tiled=True)  110 us
    all_gather x1, waiting for transfers between devices, local(): lax.all_gather(low_qkv, 'dp', axis=0, tiled=True)  61 us
  transfers between devices with their start and end apart: 12, of which 11 were waited for; matrix products, arithmetic and copies ran while one was open for 8% of the time, Pallas kernels for 0%

commit v1 on v0

--- a/solution.py
+++ b/solution.py
@@ -11,6 +11,20 @@
 RATE = 192.0
 KEEP = 0.9
 NEG = -1e30
+
+
+def match_loads(a0, axis_id):
+    lower, back = (lax.axis_size(axis_id), lax.axis_index(axis_id))
+    piece_out, r_now = (a0, 1)
+    while r_now < lower:
+        view_out = lax.ppermute(
+            piece_out, axis_id, list(map(lambda t: (t, t ^ r_now), range(lower)))
+        )
+        aux = jnp.concatenate([piece_out, view_out], 0)
+        q_next = jnp.concatenate([view_out, piece_out], 0)
+        piece_out = jnp.where(back & r_now == 0, aux, q_next)
+        r_now = 2 * r_now
+    return piece_out
 
 
 def layer_norm(value, gain, shift):
@@ -91,7 +105,7 @@
     w_qkv, w_proj, w_fc, w_down, w_norm = (
         lax.all_gather(low_qkv, "dp", axis=0, tiled=True),
         lax.all_gather(low_proj, "dp", axis=0, tiled=True),
-        lax.all_gather(low_fc, "dp", axis=0, tiled=True),
+        match_loads(low_fc, "dp"),
         lax.all_gather(low_down, "dp", axis=0, tiled=True),
         lax.all_gather(low_norm, "dp", axis=0, tiled=True),
     )

time: 2160 us -> 2170 us (level)
  waiting for transfers between devices: 1660 us -> 1550 us
  blocking collectives: 128 us -> 226 us
    ppermute x0 -> x3, waiting for transfers between devices: none -> 216 us  [match_loads(): lax.ppermute(piece_out, axis_id, list(map(lambda t: (t, t ^ r_now), range...]
    all_gather x1 -> x0, waiting for transfers between devices: 118 us -> none  [local(): lax.all_gather(low_fc, 'dp', axis=0, tiled=True)]
    all_gather x1, waiting for transfers between devices: 110 us -> 0.01 us  [local(): lax.all_gather(low_down, 'dp', axis=0, tiled=True)]
    psum x1, blocking collectives: 18.5 us -> 116 us  [local(): counts = lax.psum(local_counts, 'dp')]
    psum x3, waiting for transfers between devices: 533 us -> 436 us  [sum_over_mp(): summed = lax.psum(term_fn(0, row_count), 'mp')]
  transfers between devices with their start and end apart: 12 -> 14, of which waited for: 11 -> 11; matrix products, arithmetic and copies ran while one was open for 8% -> 9% of each run, Pallas kernels for 0% -> 0%
where the time goes in v1:
time: 2170 us; the launch traced here: 2160 us
  waiting for transfers between devices  1550 us (71%)
  blocking collectives  226 us (10%)
  matrix products  206 us (9%)
  other arithmetic  137 us (6%)
  between operations  23.3 us (1%)
    psum x3, waiting for transfers between devices, sum_over_mp(): summed = lax.psum(term_fn(0, row_count), 'mp')  436 us
    reduce_scatter x1, waiting for transfers between devices, local(): lax.psum_scatter(down_sum, 'dp', scatter_dimension=0, tiled=True)  281 us
    reduce_scatter x1, waiting for transfers between devices, local(): lax.psum_scatter(fc_sum, 'dp', scatter_dimension=0, tiled=True)  281 us
    ppermute x3, waiting for transfers between devices, match_loads(): lax.ppermute(piece_out, axis_id, list(map(lambda t: (t, t ^ r_now), range...  216 us
    reduce_scatter x1, waiting for transfers between devices, local(): lax.psum_scatter(qkv_sum, 'dp', scatter_dimension=0, tiled=True)  208 us
    psum x1, blocking collectives, local(): counts = lax.psum(local_counts, 'dp')  116 us
    all_gather x1, waiting for transfers between devices, local(): lax.all_gather(low_qkv, 'dp', axis=0, tiled=True)  61 us
  transfers between devices with their start and end apart: 14, of which 11 were waited for; matrix products, arithmetic and copies ran while one was open for 9% of the time, Pallas kernels for 0%

profile of v1, /device:TPU:0, one launch (start us, length us, event | category | flops | bytes accessed | tf_op | source)
XLA Modules:
  0.0 2164.3 jit_solution(18439398517802579553)
XLA Ops:
  19.1 32.9 %all_gather.12 = bf16[2048,6]{0,1:T(8,128)(2,1)S(1)} all-gather(bf16[256,6]{0,1:T(8,128)(2,1)S(1)} %convert_element_type.108), channel_id=1, replica_groups=mesh['dp'=8,'mp'=4] {'dp'}, dimensions={0}, use_global_device_ids=true | all-gather | bytes 27648 | tf_op jit(solution)/shard_map/all_gather | solution.py:110
  52.7 61.0 %all-gather.4.cloned.1.call-done = bf16[2048,3,512]{0,2,1:T(8,128)(2,1)} async-done(((bf16[256,3,512]{0,2,1:T(8,128)(2,1)}), bf16[2048,3,512]{0,2,1:T(8,128)(2,1)}) %all-gather.4.cloned.1.call-update) | async-done | bytes 6291472 | tf_op jit(solution)/shard_map/all_gather | solution.py:106
  140.4 23.5 %all-gather.6.cloned.1.call-done = bf16[2048,512]{1,0:T(8,128)(2,1)} async-done(((bf16[256,512]{1,0:T(8,128)(2,1)}), bf16[2048,512]{1,0:T(8,128)(2,1)}) %all-gather.6.cloned.1.call-update) | async-done | bytes 2097168 | tf_op jit(solution)/shard_map/all_gather | solution.py:107
  176.6 23.3 %collective-permute-done = bf16[256,2048]{1,0:T(8,128)(2,1)} collective-permute-done((bf16[256,2048]{1,0:T(8,128)(2,1)S(1)}, bf16[256,2048]{1,0:T(8,128)(2,1)}, u32[]{:S(2)}, u32[]{:S(2)}) %collective-permute-start) | collective-permute-done | bytes 1048608 | tf_op jit(solution)/shard_map/ppermute | solution.py:20
  205.5 44.1 %collective-permute-done.1 = bf16[512,2048]{1,0:T(8,128)(2,1)} collective-permute-done((bf16[512,2048]{1,0:T(8,128)(2,1)}, bf16[512,2048]{1,0:T(8,128)(2,1)}, u32[]{:S(2)}, u32[]{:S(2)}) %collective-permute-start.1) | collective-permute-done | bytes 2097184 | tf_op jit(solution)/shard_map/ppermute | solution.py:20
  260.0 116.4 %psum.58 = f32[4]{0:T(128)S(1)} all-reduce(f32[4]{0:T(128)S(1)} %fusion.46), channel_id=1, replica_groups=mesh['dp'=8,'mp'=4] {'dp'}, use_global_device_ids=true, to_apply=%region_9.10 | all-reduce | flops 4 | bytes 32 | tf_op jit(solution)/shard_map/psum | solution.py:90
  390.3 148.6 %collective-permute-done.2 = bf16[1024,2048]{1,0:T(8,128)(2,1)} collective-permute-done((bf16[1024,2048]{1,0:T(8,128)(2,1)}, bf16[1024,2048]{1,0:T(8,128)(2,1)}, u32[]{:S(2)}, u32[]{:S(2)}) %collective-permute-start.2) | collective-permute-done | bytes 4194336 | tf_op jit(solution)/shard_map/ppermute | solution.py:20
  538.9 17.3 fusion.37
  556.2 23.0 %convert_reduce_fusion.1 = (f32[2048]{0:T(1024)}, bf16[1024,2048]{1,0:T(8,128)(2,1)}) fusion(bf16[2048,2048]{1,0:T(8,128)(2,1)} %all-gather.8.cloned.1.call-done, bf16[1024,2048]{1,0:T(8,128)(2,1)} %param.27, f32[1024]{0:T(1024)S(1)} %fusion.43, f32[1024,2048]{1,0:T(8,128)} %fusion.37, f32[2048]{0:T(1024)S(1)} %copy-done.49), kind=kOutput, calls=%fused_computation.35 | convolution fusion | flops 8652847104 | bytes 25186304 | tf_op jit(solution)/shard_map/td,df->tf/dot_general | solution.py:165
  579.2 19.3 fusion.36
  598.5 17.5 fusion.53
  616.0 157.7 %all-reduce.8.cloned.1.call-done = f32[1024,2048]{1,0:T(8,128)} async-done(((f32[1024,2048]{1,0:T(8,128)}), f32[1024,2048]{1,0:T(8,128)}) %all-reduce.8.cloned.1.call-update) | async-done | bytes 8388624 | tf_op jit(solution)/shard_map/psum | solution.py:84
  803.0 12.6 multiply_reduce_fusion
  815.6 12.1 multiply_convert_fusion
  857.2 278.3 %all-reduce.10.cloned.1.call-done = (f32[1024,2048]{1,0:T(8,128)}, f32[1024,2048]{1,0:T(8,128)}) async-done(((f32[1024,2048]{1,0:T(8,128)}, f32[1024,2048]{1,0:T(8,128)}), (f32[1024,2048]{1,0:T(8,128)}, f32[1024,2048]{1,0:T(8,128)})) %all-reduce.10.cloned.1.call-update) | async-done | bytes 16777232 | tf_op jit(solution)/shard_map/psum | solution.py:84
  1159.0 13.6 fusion.38
  1173.3 16.4 fusion.54
  1190.0 17.1 fusion.27
  1207.8 37.8 %all-reduce = (f32[2,512]{1,0:T(2,128)S(1)}, f32[2048]{0:T(1024)S(1)}) all-reduce(f32[2,512]{1,0:T(2,128)S(1)} %convert_reduce_fusion.2, f32[2048]{0:T(1024)S(1)} %copy-done.48), channel_id=1, replica_groups=mesh['dp'=8,'mp'=4] {'dp'}, use_global_device_ids=true, to_apply=%region_28.29 | all-reduce | flops 3072 | bytes 24576 | tf_op jit(solution)/shard_map/psum | solution.py:245
  1251.9 41.6 %reduce-scatter.6.cloned.1.call-done = f32[256,6]{0,1:T(8,128)} async-done(((f32[2048,6]{0,1:T(8,128)}), f32[256,6]{0,1:T(8,128)}) %reduce-scatter.6.cloned.1.call-update) | async-done | bytes 6160 | tf_op jit(solution)/shard_map/reduce_scatter | solution.py:243
  1296.1 208.2 %reduce-scatter.8.cloned.1.call-done = f32[256,3,512]{2,0,1:T(8,128)} async-done(((f32[2048,3,512]{2,0,1:T(8,128)}), f32[256,3,512]{2,0,1:T(8,128)}) %reduce-scatter.8.cloned.1.call-update) | async-done | bytes 1572880 | tf_op jit(solution)/shard_map/reduce_scatter | solution.py:239
  1508.7 280.9 %reduce-scatter.12.cloned.1.call-done = f32[256,2048]{1,0:T(8,128)} async-done(((f32[2048,2048]{1,0:T(8,128)}), f32[256,2048]{1,0:T(8,128)}) %reduce-scatter.12.cloned.1.call-update) | async-done | bytes 2097168 | tf_op jit(solution)/shard_map/reduce_scatter | solution.py:241
  1793.7 281.4 %reduce-scatter.14.cloned.1.call-done = f32[256,2048]{1,0:T(8,128)} async-done(((f32[2048,2048]{1,0:T(8,128)}), f32[256,2048]{1,0:T(8,128)}) %reduce-scatter.14.cloned.1.call-update) | async-done | bytes 2097168 | tf_op jit(solution)/shard_map/reduce_scatter | solution.py:242
  2089.4 39.1 %psum.63 = f32[]{:T(128)} all-reduce(f32[]{:T(128)S(6)} %add.249), channel_id=1, replica_groups=mesh['dp'=8,'mp'=4] {'dp','mp'}, use_global_device_ids=true, to_apply=%region_41.42 | all-reduce | flops 1 | bytes 8 | tf_op jit(solution)/shard_map/psum | solution.py:263
  (215 shorter events, 217.1 us)
Async XLA Ops:
  7.2 106.5 %all-gather.4.cloned.1.call-start = ((), (), s32[]{:S(2)}) async-start(), calls=%async_computation.5 | async-start | bytes 7077888 | tf_op jit(solution)/shard_map/all_gather | solution.py:106
  9.9 154.1 %all-gather.6.cloned.1.call-start = ((), (), s32[]{:S(2)}) async-start(), calls=%async_computation.6 | async-start | bytes 2359296 | tf_op jit(solution)/shard_map/all_gather | solution.py:107
  11.7 368.5 %all-reduce.6.cloned.1.call-start = ((), (), s32[]{:S(2)}) async-start(), calls=%async_computation.7 | async-start | bytes 16777216 | tf_op jit(solution)/shard_map/psum | solution.py:84
  15.6 109.2 %copy-start.28 = (f32[1024]{0:T(1024)}, f32[1024]{0:T(1024)S(1)}, u32[]{:S(2)}) copy-start(f32[1024]{0:T(1024)S(1)} %broadcast_multiply_fusion.8) | copy-start | bytes 12292
  19.0 105.8 %copy-start.32 = (f32[1024]{0:T(1024)}, f32[1024]{0:T(1024)S(1)}, u32[]{:S(2)}) copy-start(f32[1024]{0:T(1024)S(1)} %fusion.15) | copy-start | bytes 12292
  19.1 105.8 %copy-start.30 = (f32[1024]{0:T(1024)}, f32[1024]{0:T(1024)S(1)}, u32[]{:S(2)}) copy-start(f32[1024]{0:T(1024)S(1)} %fusion.44) | copy-start | bytes 12292
  52.6 486.3 %copy-start.44 = (f32[2048,1]{0,1:T(1,128)}, f32[2048,1]{0,1:T(1,128)S(1)}, u32[]{:S(2)}) copy-start(f32[2048,1]{0,1:T(1,128)S(1)} %get-tuple-element.121) | copy-start | bytes 24580
  171.4 384.8 %all-gather.8.cloned.1.call-start = ((), (), s32[]{:S(2)}) async-start(), calls=%async_computation.8 | async-start | bytes 9437184 | tf_op jit(solution)/shard_map/all_gather | solution.py:109
  174.2 202.2 %copy-start.54 = (s32[4]{0:T(128)S(1)}, s32[4]{0:T(128)}, u32[]{:S(2)}) copy-start(s32[4]{0:T(128)} %param.30) | copy-start | bytes 52
  174.2 599.5 %all-reduce.8.cloned.1.call-start = ((), (), s32[]{:S(2)}) async-start(), calls=%async_computation.9 | async-start | bytes 16777216 | tf_op jit(solution)/shard_map/psum | solution.py:84
  176.5 23.5 %collective-permute-start = (bf16[256,2048]{1,0:T(8,128)(2,1)S(1)}, bf16[256,2048]{1,0:T(8,128)(2,1)}, u32[]{:S(2)}, u32[]{:S(2)}) collective-permute-start(bf16[256,2048]{1,0:T(8,128)(2,1)S(1)} %convert_element_type.118), channel_id=1, source_target_pairs={{0,4},{4,0},{8,12},{12,8},{16,20},{20,16},{24,28},{28,24},{1,5},{5... | collective-permute-start | bytes 3145736 | tf_op jit(solution)/shard_map/ppermute | solution.py:20
  203.7 45.9 %collective-permute-start.1 = (bf16[512,2048]{1,0:T(8,128)(2,1)}, bf16[512,2048]{1,0:T(8,128)(2,1)}, u32[]{:S(2)}, u32[]{:S(2)}) collective-permute-start(bf16[512,2048]{1,0:T(8,128)(2,1)} %maximum_select_fusion.2), channel_id=1, source_target_pairs={{0,8},{4,12},{8,0},{12,4},{16,24},{20,28},{24,16},{28,20},{1,9},{5... | collective-permute-start | bytes 6291464 | tf_op jit(solution)/shard_map/ppermute | solution.py:20
  255.7 283.1 %collective-permute-start.2 = (bf16[1024,2048]{1,0:T(8,128)(2,1)}, bf16[1024,2048]{1,0:T(8,128)(2,1)}, u32[]{:S(2)}, u32[]{:S(2)}) collective-permute-start(bf16[1024,2048]{1,0:T(8,128)(2,1)} %maximum_select_fusion.1), channel_id=1, source_target_pairs={{0,16},{4,20},{8,24},{12,28},{16,0},{20,4},{24,8},{28,12},{1,17},{... | collective-permute-start | bytes 12582920 | tf_op jit(solution)/shard_map/ppermute | solution.py:20
  598.5 537.0 %all-reduce.10.cloned.1.call-start = ((), (), s32[]{:S(2)}) async-start(), calls=%async_computation.15 | async-start | bytes 33554432 | tf_op jit(solution)/shard_map/psum | solution.py:84
  846.4 289.2 %copy-start.27 = (f32[2048,1]{0,1:T(1,128)S(1)}, f32[2048,1]{0,1:T(1,128)}, u32[]{:S(2)}) copy-start(f32[2048,1]{0,1:T(1,128)} %copy-done.26) | copy-start | bytes 24580
  846.4 289.1 %copy-start.29 = (f32[1024]{0:T(1024)S(1)}, f32[1024]{0:T(1024)}, u32[]{:S(2)}) copy-start(f32[1024]{0:T(1024)} %copy-done.28) | copy-start | bytes 12292
  846.4 403.0 %reduce-scatter.10.cloned.1.call-start = ((), (), s32[]{:S(2)}) async-start(), calls=%async_computation.12 | async-start | bytes 4718592 | tf_op jit(solution)/shard_map/reduce_scatter | solution.py:240
  857.1 284.8 %copy-start.33 = (f32[1024]{0:T(1024)S(1)}, f32[1024]{0:T(1024)}, u32[]{:S(2)}) copy-start(f32[1024]{0:T(1024)} %copy-done.32) | copy-start | bytes 12292
  857.1 284.8 %copy-start.31 = (f32[1024]{0:T(1024)S(1)}, f32[1024]{0:T(1024)}, u32[]{:S(2)}) copy-start(f32[1024]{0:T(1024)} %copy-done.30) | copy-start | bytes 12292
  857.1 436.4 %reduce-scatter.6.cloned.1.call-start = ((), (), s32[]{:S(2)}) async-start(), calls=%async_computation.10 | async-start | bytes 73728 | tf_op jit(solution)/shard_map/reduce_scatter | solution.py:243
  1158.8 345.6 %reduce-scatter.8.cloned.1.call-start = ((), (), s32[]{:S(2)}) async-start(), calls=%async_computation.11 | async-start | bytes 14155776 | tf_op jit(solution)/shard_map/reduce_scatter | solution.py:239
  1172.6 617.0 %reduce-scatter.12.cloned.1.call-start = ((), (), s32[]{:S(2)}) async-start(), calls=%async_computation.13 | async-start | bytes 18874368 | tf_op jit(solution)/shard_map/reduce_scatter | solution.py:241
  1189.7 885.3 %reduce-scatter.14.cloned.1.call-start = ((), (), s32[]{:S(2)}) async-start(), calls=%async_computation.14 | async-start | bytes 18874368 | tf_op jit(solution)/shard_map/reduce_scatter | solution.py:242
  1207.1 872.0 %copy-start.34 = (f32[2048,1]{0,1:T(1,128)S(1)}, f32[2048,1]{0,1:T(1,128)}, u32[]{:S(2)}) copy-start(f32[2048,1]{0,1:T(1,128)} %get-tuple-element.119) | copy-start | bytes 24580
  (47 other events, 1049.4 us)
Sparse Core Ops, SparseCore 0:
  10.7 102.9 all-gather.3
  116.4 47.5 all-gather.5
  171.5 151.3 all-reduce.5
  325.4 183.7 all-gather.7
  598.6 175.0 all-reduce.7
  846.5 288.9 all-reduce.9
  1139.7 88.2 reduce-scatter.9
  1232.4 61.1 reduce-scatter.5
  1297.6 206.7 reduce-scatter.7
  1508.5 281.1 reduce-scatter.11
  1793.4 281.5 reduce-scatter.13
